TPU v7x, 32 devices: a whole 2x2x4 slice. The times are simulated.
32 devices in a mesh: domain: 8 (over z, y), vec: 4 (over x, core).
Axes of the slice: x: 2, y: 2, z: 4, core: 2. Of those that a mesh axis runs over, the one named last changes fastest.
Arguments:
- vectors: float32 [4096, 512], P('domain', 'vec'), may hold values from -6 to 6
- hamiltonian: float32 [512, 128, 128], P('domain'), may hold values from -0.09375 to 0.09375
- tile_pairs: int32 [512, 2], P('domain'), may hold values from 0 to 31, as said below
- tile_counts: int32 [8], P('domain'), may hold values from 8 to 64, as said below
Outputs:
- filtered: float32 [4096, 512], P('domain', 'vec')
- gram: float32 [512, 512], P('vec')
Inputs may be any that keep to these rules, and one draw needn't show every extreme that they name: `tile_pairs`: slots k * 64 to (k + 1) * 64 - 1 have their row group r among groups k * 4 to (k + 1) * 4 - 1 and their column group c with r <= c <= min(k * 4 + 3 * 4 - 1, 31); pairs may repeat, and repeated blocks add. `tile_counts`: one domain index uses all 64 slots.
All inputs are finite; a program needn't handle non-finite values.
Results may differ from a plain program's by a relative error of at most 0.0003.
Values sent between devices are 32-bit elements; how exact they have to be, the bound alone decides.
A program may use at most 64 MiB of HBM per device.

v0:
```python
import jax
import jax.numpy as jnp
from jax import lax
from jax.sharding import PartitionSpec as P

TILE = 128
REACH = 2
center_shift = 1.0
half_width = 1.5


def from_behind(block, axis, distance):
    devices = range(lax.axis_size(axis))
    route = [(i - distance, i) for i in devices if i - distance in devices]
    return lax.ppermute(block, axis, route)


def local_products(own, window, tiles, row_loc, col_loc, count, groups):
    block_slots = 8
    width = own.shape[2]
    span = window.shape[0]
    n_blocks = (count + block_slots - 1) // block_slots

    def block_step(index, carry):
        rows_acc, back_acc = carry
        start = index * block_slots
        tile = lax.dynamic_slice_in_dim(tiles, start, block_slots, 0)
        rloc = lax.dynamic_slice_in_dim(row_loc, start, block_slots, 0)
        cloc = lax.dynamic_slice_in_dim(col_loc, start, block_slots, 0)
        used = (start + jnp.arange(block_slots, dtype=jnp.int32) < count).astype(jnp.float32)
        apart = (rloc != cloc).astype(jnp.float32)
        fwd = jnp.einsum("tij,tjc->tic", tile, window[cloc], precision=lax.Precision.HIGHEST)
        back = jnp.einsum("tji,tjc->tic", tile, own[rloc], precision=lax.Precision.HIGHEST)
        row_hot = (rloc[:, None] == jnp.arange(groups, dtype=jnp.int32)[None, :]).astype(
            jnp.float32
        ) * used[:, None]
        col_hot = (cloc[:, None] == jnp.arange(span, dtype=jnp.int32)[None, :]).astype(
            jnp.float32
        ) * (used * apart)[:, None]
        rows_acc = rows_acc + jnp.einsum(
            "tg,tic->gic", row_hot, fwd, precision=lax.Precision.HIGHEST
        )
        back_acc = back_acc + jnp.einsum(
            "tg,tic->gic", col_hot, back, precision=lax.Precision.HIGHEST
        )
        return (rows_acc, back_acc)

    start_rows = jnp.zeros((groups, TILE, width), jnp.float32)
    start_back = jnp.zeros((span, TILE, width), jnp.float32)
    return lax.fori_loop(0, n_blocks, block_step, (start_rows, start_back))


def apply_ham(block, tiles, row_loc, col_loc, count):
    groups = block.shape[0] // TILE
    width = block.shape[1]
    own = block.reshape(groups, TILE, width)
    pieces = [own]
    for step in range(1, REACH + 1):
        pieces.append(from_behind(own, "domain", -step))
    window = jnp.concatenate(pieces, 0)
    rows_acc, back_acc = local_products(own, window, tiles, row_loc, col_loc, count, groups)
    result = rows_acc + back_acc[:groups]
    for step in range(1, REACH + 1):
        result = result + from_behind(back_acc[step * groups : (step + 1) * groups], "domain", step)
    return result.reshape(groups * TILE, width)


def shards(vectors, hamiltonian, tile_pairs, tile_counts):
    groups = vectors.shape[0] // TILE
    base = lax.axis_index("domain") * groups
    count = tile_counts[0]
    diag = tile_pairs[:, 0] == tile_pairs[:, 1]
    tiles = jnp.where(
        diag[:, None, None], 0.5 * (hamiltonian + jnp.swapaxes(hamiltonian, 1, 2)), hamiltonian
    )
    row_loc = tile_pairs[:, 0] - base
    col_loc = tile_pairs[:, 1] - base
    second = (
        apply_ham(vectors, tiles, row_loc, col_loc, count) - center_shift * vectors
    ) / half_width
    third = (
        2.0
        * (apply_ham(second, tiles, row_loc, col_loc, count) - center_shift * second)
        / half_width
        - vectors
    )
    filtered = (
        2.0 * (apply_ham(third, tiles, row_loc, col_loc, count) - center_shift * third) / half_width
        - second
    )
    total_rows = vectors.shape[0] * lax.axis_size("domain")
    gathered = lax.all_gather(filtered, "vec", axis=1, tiled=True)
    partial_block = (
        jnp.dot(
            filtered.T,
            gathered,
            precision=lax.Precision.HIGHEST,
            preferred_element_type=jnp.float32,
        )
        / total_rows
    )
    gram = lax.psum(partial_block, "domain")
    return (filtered, gram)


def solution(mesh):
    in_specs = (P("domain", "vec"), P("domain", None, None), P("domain", None), P("domain"))
    out_specs = (P("domain", "vec"), P("vec", None))
    return jax.shard_map(shards, mesh=mesh, in_specs=in_specs, out_specs=out_specs, check_vma=False)
```

profile of v0, /device:TPU:0, one launch (start us, length us, event | category | flops | bytes accessed | tf_op | source)
XLA Modules:
  0.0 392.4 jit_solution(13187985193437510828)
XLA Ops:
  9.8 5.6 %copy.6 = f32[64,128,128]{1,2,0:T(8,128)} copy(f32[64,128,128]{2,1,0:T(8,128)} %param.11) | data formatting | bytes 8388608 | tf_op args[1]
  15.4 5.9 %fusion.61 = f32[64,128,128]{2,1,0:T(8,128)} fusion(f32[64,128,128]{2,1,0:T(8,128)} %param.11, f32[64,128,128]{1,2,0:T(8,128)} %copy.6, pred[64]{0:T(512)(128)(4,1)S(1)} %compare_bitcast_fusion), kind=kLoop, calls=%fused_computation.98 | loop fusion | flops 3145728 | bytes 12582976 | tf_op jit(solution)/shard_map/jit(_where)/select_n | solution.py:73
  22.3 24.5 %while.36 = (s32[]{:T(128)}, f32[4,128,128]{2,0,1:T(4,128)S(1)}, f32[12,128,128]{2,0,1:T(8,128)S(1)}, s32[]{:T(128)}, s32[64]{0:T(128)S(1)}, /*index=5*/s32[]{:T...) while((s32[]{:T(128)}, f32[4,128,128]{2,0,1:T(4,128)S(1)}, ...), condition=%wide.region_1.2_spmd, body=%wide.region_0.1_spmd.sunk | while | flops 428083552 | bytes 8397583 | solution.py:50
  23.6 1.7 fusion.116
  26.9 2.1 fusion.117
  29.0 1.5 convolution_add_fusion.13
  31.8 1.7 fusion.116
  35.1 2.1 fusion.117
  37.1 1.5 convolution_add_fusion.13
  40.0 1.7 fusion.116
  43.2 2.1 fusion.117
  45.3 1.5 convolution_add_fusion.13
  46.9 1.3 collective-permute-start.3
  48.2 5.6 %collective-permute-start.2 = (f32[4,128,128]{2,0,1:T(4,128)S(1)}, f32[4,128,128]{2,0,1:T(4,128)S(1)}, u32[]{:S(2)}, u32[]{:S(2)}) collective-permute-start(f32[4,128,128]{2,0,1:T(4,128)S(1)} %get-tuple-element.252), channel_id=1, source_target_pairs={{0,4},{4,8},{8,12},{12,16},{16,20},{20,24},{24,28},{1,5},{5,9},{9,... | collective-permute-start | bytes 786440 | tf_op jit(solution)/shard_map/ppermute | solution.py:15
  54.7 4.6 %collective-permute-done.2 = f32[4,128,128]{2,0,1:T(4,128)S(1)} collective-permute-done((f32[4,128,128]{2,0,1:T(4,128)S(1)}, f32[4,128,128]{2,0,1:T(4,128)S(1)}, u32[]{:S(2)}, u32[]{:S(2)}) %collective-permute-start.2) | collective-permute-done | bytes 262176 | tf_op jit(solution)/shard_map/ppermute | solution.py:15
  59.5 1.3 collective-permute-start.5
  62.1 51.8 %collective-permute-done.5 = f32[4,128,128]{2,1,0:T(8,128)S(1)} collective-permute-done((f32[4,128,128]{2,1,0:T(8,128)S(1)}, f32[4,128,128]{2,1,0:T(8,128)S(1)}, u32[]{:S(2)}, u32[]{:S(2)}) %collective-permute-start.5) | collective-permute-done | bytes 262176 | tf_op jit(solution)/shard_map/ppermute | solution.py:15
  114.1 24.5 %while.37 = (s32[]{:T(128)}, f32[4,128,128]{2,0,1:T(4,128)S(1)}, f32[12,128,128]{2,0,1:T(8,128)S(1)}, s32[]{:T(128)}, s32[64]{0:T(128)S(1)}, /*index=5*/s32[]{:T...) while((s32[]{:T(128)}, f32[4,128,128]{2,0,1:T(4,128)S(1)}, ...), condition=%wide.region_3.4_spmd, body=%wide.region_2.3_spmd.sunk | while | flops 428083552 | bytes 8397583 | solution.py:50
  115.4 1.7 fusion.126
  118.7 2.1 fusion.127
  120.8 1.5 convolution_add_fusion.15
  123.6 1.7 fusion.126
  126.9 2.1 fusion.127
  128.9 1.5 convolution_add_fusion.15
  131.8 1.7 fusion.126
  135.0 2.1 fusion.127
  137.1 1.5 convolution_add_fusion.15
  138.7 1.3 collective-permute-start.7
  140.0 6.4 %collective-permute-start.6 = (f32[4,128,128]{2,0,1:T(4,128)S(1)}, f32[4,128,128]{2,0,1:T(4,128)S(1)}, u32[]{:S(2)}, u32[]{:S(2)}) collective-permute-start(f32[4,128,128]{2,0,1:T(4,128)S(1)} %get-tuple-element.250), channel_id=1, source_target_pairs={{0,4},{4,8},{8,12},{12,16},{16,20},{20,24},{24,28},{1,5},{5,9},{9,... | collective-permute-start | bytes 786440 | tf_op jit(solution)/shard_map/ppermute | solution.py:15
  146.5 3.8 collective-permute-done.6
  153.2 54.4 %collective-permute-done.9 = f32[4,128,128]{2,1,0:T(8,128)S(1)} collective-permute-done((f32[4,128,128]{2,1,0:T(8,128)S(1)}, f32[4,128,128]{2,1,0:T(8,128)S(1)}, u32[]{:S(2)}, u32[]{:S(2)}) %collective-permute-start.9) | collective-permute-done | bytes 262176 | tf_op jit(solution)/shard_map/ppermute | solution.py:15
  207.7 24.7 %while.38 = (s32[]{:T(128)}, f32[4,128,128]{2,0,1:T(4,128)S(1)}, f32[12,128,128]{2,0,1:T(8,128)S(1)}, s32[]{:T(128)}, s32[64]{0:T(128)S(1)}, /*index=5*/s32[]{:T...) while((s32[]{:T(128)}, f32[4,128,128]{2,0,1:T(4,128)S(1)}, ...), condition=%wide.region_5.6_spmd, body=%wide.region_4.5_spmd.sunk | while | flops 428083552 | bytes 8397583 | solution.py:50
  209.3 1.7 fusion.136
  212.5 2.1 fusion.137
  214.6 1.5 convolution_add_fusion.17
  217.4 1.7 fusion.136
  220.7 2.1 fusion.137
  222.8 1.5 convolution_add_fusion.17
  225.6 1.7 fusion.136
  228.9 2.1 fusion.137
  230.9 1.5 convolution_add_fusion.17
  232.5 1.3 collective-permute-start.11
  233.9 6.2 %collective-permute-start.10 = (f32[4,128,128]{2,0,1:T(4,128)S(1)}, f32[4,128,128]{2,0,1:T(4,128)S(1)}, u32[]{:S(2)}, u32[]{:S(2)}) collective-permute-start(f32[4,128,128]{2,0,1:T(4,128)S(1)} %get-tuple-element.248), channel_id=1, source_target_pairs={{0,4},{4,8},{8,12},{12,16},{16,20},{20,24},{24,28},{1,5},{5,9},{9,... | collective-permute-start | bytes 786440 | tf_op jit(solution)/shard_map/ppermute | solution.py:15
  240.1 3.8 collective-permute-done.10
  244.9 64.1 %all-gather.2.cloned.1.call-done = f32[512,512]{1,0:T(8,128)} async-done(((f32[512,128]{1,0:T(8,128)}), f32[512,512]{1,0:T(8,128)}) %all-gather.2.cloned.1.call-update) | async-done | bytes 1048592 | tf_op jit(solution)/shard_map/all_gather | solution.py:92
  308.9 2.8 convolution_multiply_fusion
  311.7 72.2 %all-reduce.2.cloned.1.call-done = f32[128,512]{1,0:T(8,128)} async-done(((f32[128,512]{1,0:T(8,128)}), f32[128,512]{1,0:T(8,128)}) %all-reduce.2.cloned.1.call-update) | async-done | bytes 262160 | tf_op jit(solution)/shard_map/psum | solution.py:102
  383.9 1.7 copy.69
  (106 shorter events, 35.2 us)
Async XLA Ops:
  7.2 301.8 %all-gather.2.cloned.1.call-start = ((), (), s32[]{:S(2)}) async-start(), calls=%async_computation | async-start | bytes 1310720 | tf_op jit(solution)/shard_map/all_gather | solution.py:92
  7.2 8.2 %copy-start.1 = (s32[64,2]{0,1:T(2,128)S(1)}, s32[64,2]{0,1:T(2,128)}, u32[]{:S(2)}) copy-start(s32[64,2]{0,1:T(2,128)} %param.12) | copy-start | bytes 1540
  7.2 14.9 %collective-permute-start.1 = (f32[4,128,128]{2,1,0:T(8,128)}, f32[4,128,128]{2,1,0:T(8,128)S(1)}, u32[]{:S(2)}, u32[]{:S(2)}) collective-permute-start(f32[4,128,128]{2,1,0:T(8,128)} %bitcast.89), channel_id=1, source_target_pairs={{8,0},{12,4},{16,8},{20,12},{24,16},{28,20},{9,1},{13,5},{17,9},{2... | collective-permute-start | bytes 786440 | tf_op jit(solution)/shard_map/ppermute | solution.py:15
  8.5 13.6 %collective-permute-start = (f32[4,128,128]{2,1,0:T(8,128)}, f32[4,128,128]{2,1,0:T(8,128)S(1)}, u32[]{:S(2)}, u32[]{:S(2)}) collective-permute-start(f32[4,128,128]{2,1,0:T(8,128)} %bitcast.90), channel_id=1, source_target_pairs={{4,0},{8,4},{12,8},{16,12},{20,16},{24,20},{28,24},{5,1},{9,5},{13... | collective-permute-start | bytes 786440 | tf_op jit(solution)/shard_map/ppermute | solution.py:15
  15.4 6.7 %copy-start = (f32[512,128]{1,0:T(8,128)S(1)}, f32[512,128]{1,0:T(8,128)}, u32[]{:S(2)}) copy-start(f32[512,128]{1,0:T(8,128)} %param.10) | copy-start | bytes 786436
  46.9 7.8 %collective-permute-start.3 = (f32[4,128,128]{2,0,1:T(4,128)S(1)}, f32[4,128,128]{2,0,1:T(4,128)S(1)}, u32[]{:S(2)}, u32[]{:S(2)}) collective-permute-start(f32[4,128,128]{2,0,1:T(4,128)S(1)} %get-tuple-element.253), channel_id=1, source_target_pairs={{0,8},{4,12},{8,16},{12,20},{16,24},{20,28},{1,9},{5,13},{9,17},{1... | collective-permute-start | bytes 786440 | tf_op jit(solution)/shard_map/ppermute | solution.py:15
  48.2 11.1 %collective-permute-start.2 = (f32[4,128,128]{2,0,1:T(4,128)S(1)}, f32[4,128,128]{2,0,1:T(4,128)S(1)}, u32[]{:S(2)}, u32[]{:S(2)}) collective-permute-start(f32[4,128,128]{2,0,1:T(4,128)S(1)} %get-tuple-element.252), channel_id=1, source_target_pairs={{0,4},{4,8},{8,12},{12,16},{16,20},{20,24},{24,28},{1,5},{5,9},{9,... | collective-permute-start | bytes 786440 | tf_op jit(solution)/shard_map/ppermute | solution.py:15
  59.5 54.4 %collective-permute-start.5 = (f32[4,128,128]{2,1,0:T(8,128)S(1)}, f32[4,128,128]{2,1,0:T(8,128)S(1)}, u32[]{:S(2)}, u32[]{:S(2)}) collective-permute-start(f32[4,128,128]{2,1,0:T(8,128)S(1)} %bitcast.83), channel_id=1, source_target_pairs={{8,0},{12,4},{16,8},{20,12},{24,16},{28,20},{9,1},{13,5},{17,9},{2... | collective-permute-start | bytes 786440 | tf_op jit(solution)/shard_map/ppermute | solution.py:15
  60.8 53.1 %collective-permute-start.4 = (f32[4,128,128]{2,1,0:T(8,128)S(1)}, f32[4,128,128]{2,1,0:T(8,128)S(1)}, u32[]{:S(2)}, u32[]{:S(2)}) collective-permute-start(f32[4,128,128]{2,1,0:T(8,128)S(1)} %bitcast.84), channel_id=1, source_target_pairs={{4,0},{8,4},{12,8},{16,12},{20,16},{24,20},{28,24},{5,1},{9,5},{13... | collective-permute-start | bytes 786440 | tf_op jit(solution)/shard_map/ppermute | solution.py:15
  138.7 7.8 %collective-permute-start.7 = (f32[4,128,128]{2,0,1:T(4,128)S(1)}, f32[4,128,128]{2,0,1:T(4,128)S(1)}, u32[]{:S(2)}, u32[]{:S(2)}) collective-permute-start(f32[4,128,128]{2,0,1:T(4,128)S(1)} %get-tuple-element.251), channel_id=1, source_target_pairs={{0,8},{4,12},{8,16},{12,20},{16,24},{20,28},{1,9},{5,13},{9,17},{1... | collective-permute-start | bytes 786440 | tf_op jit(solution)/shard_map/ppermute | solution.py:15
  140.0 10.3 %collective-permute-start.6 = (f32[4,128,128]{2,0,1:T(4,128)S(1)}, f32[4,128,128]{2,0,1:T(4,128)S(1)}, u32[]{:S(2)}, u32[]{:S(2)}) collective-permute-start(f32[4,128,128]{2,0,1:T(4,128)S(1)} %get-tuple-element.250), channel_id=1, source_target_pairs={{0,4},{4,8},{8,12},{12,16},{16,20},{20,24},{24,28},{1,5},{5,9},{9,... | collective-permute-start | bytes 786440 | tf_op jit(solution)/shard_map/ppermute | solution.py:15
  150.6 57.0 %collective-permute-start.9 = (f32[4,128,128]{2,1,0:T(8,128)S(1)}, f32[4,128,128]{2,1,0:T(8,128)S(1)}, u32[]{:S(2)}, u32[]{:S(2)}) collective-permute-start(f32[4,128,128]{2,1,0:T(8,128)S(1)} %bitcast.95), channel_id=1, source_target_pairs={{8,0},{12,4},{16,8},{20,12},{24,16},{28,20},{9,1},{13,5},{17,9},{2... | collective-permute-start | bytes 786440 | tf_op jit(solution)/shard_map/ppermute | solution.py:15
  151.9 55.7 %collective-permute-start.8 = (f32[4,128,128]{2,1,0:T(8,128)S(1)}, f32[4,128,128]{2,1,0:T(8,128)S(1)}, u32[]{:S(2)}, u32[]{:S(2)}) collective-permute-start(f32[4,128,128]{2,1,0:T(8,128)S(1)} %bitcast.96), channel_id=1, source_target_pairs={{4,0},{8,4},{12,8},{16,12},{20,16},{24,20},{28,24},{5,1},{9,5},{13... | collective-permute-start | bytes 786440 | tf_op jit(solution)/shard_map/ppermute | solution.py:15
  232.5 7.5 %collective-permute-start.11 = (f32[4,128,128]{2,0,1:T(4,128)S(1)}, f32[4,128,128]{2,0,1:T(4,128)S(1)}, u32[]{:S(2)}, u32[]{:S(2)}) collective-permute-start(f32[4,128,128]{2,0,1:T(4,128)S(1)} %get-tuple-element.249), channel_id=1, source_target_pairs={{0,8},{4,12},{8,16},{12,20},{16,24},{20,28},{1,9},{5,13},{9,17},{1... | collective-permute-start | bytes 786440 | tf_op jit(solution)/shard_map/ppermute | solution.py:15
  233.9 10.1 %collective-permute-start.10 = (f32[4,128,128]{2,0,1:T(4,128)S(1)}, f32[4,128,128]{2,0,1:T(4,128)S(1)}, u32[]{:S(2)}, u32[]{:S(2)}) collective-permute-start(f32[4,128,128]{2,0,1:T(4,128)S(1)} %get-tuple-element.248), channel_id=1, source_target_pairs={{0,4},{4,8},{8,12},{12,16},{16,20},{20,24},{24,28},{1,5},{5,9},{9,... | collective-permute-start | bytes 786440 | tf_op jit(solution)/shard_map/ppermute | solution.py:15
  244.8 139.1 %all-reduce.2.cloned.1.call-start = ((), (), s32[]{:S(2)}) async-start(), calls=%async_computation.1 | async-start | bytes 524288 | tf_op jit(solution)/shard_map/psum | solution.py:102
Sparse Core Ops, SparseCore 0:
  244.9 63.9 all-gather.1
  312.8 71.0 all-reduce.1
where the time goes:
time: 395 us; the launch traced here: 392 us
  waiting for transfers between devices  256 us (65%)
  matrix products  58.6 us (15%)
  starting transfers between devices  30 us (8%)
  local copies, waits for them, and re-layouts  18.4 us (5%)
  between operations  15 us (4%)
  other arithmetic  14 us (4%)
    ppermute x12, waiting for transfers between devices, from_behind(): return lax.ppermute(block, axis, route)  119 us
    psum x1, waiting for transfers between devices, shards(): gram = lax.psum(partial_block, 'domain')  72.2 us
    all_gather x1, waiting for transfers between devices, shards(): gathered = lax.all_gather(filtered, 'vec', axis=1, tiled=True)  64.1 us
    ppermute x12, starting transfers between devices, from_behind(): return lax.ppermute(block, axis, route)  29.9 us
    dot_general x9, matrix products, block_step(): jnp.einsum('tji,tjc->tic', tile, own[rloc], precision=lax.Precision.HIGHEST)  18.5 us
    dot_general x9, matrix products, block_step(): jnp.einsum('tij,tjc->tic', tile, window[cloc], precision=lax.Precision.HI...  15.2 us
    dot_general x9, matrix products, block_step(): jnp.einsum('tg,tic->gic', col_hot, back, precision=lax.Precision.HIGHEST)  13.5 us
    dot_general x9, matrix products, block_step(): jnp.einsum('tg,tic->gic', row_hot, fwd, precision=lax.Precision.HIGHEST)  8.57 us
  transfers between devices with their start and end apart: 14, of which 8 were waited for; matrix products, arithmetic and copies ran while one was open for 3% of the time, Pallas kernels for 0%

commit v1 on v0

--- a/solution.py
+++ b/solution.py
@@ -99,7 +99,7 @@
         )
         / total_rows
     )
-    gram = lax.psum(partial_block, "domain")
+    gram = jnp.sum(lax.all_gather(partial_block, "domain"), axis=0)
     return (filtered, gram)
 
 

time: 395 us -> 373 us (0.944)
  waiting for transfers between devices: 256 us -> 233 us
    psum x1 -> x0, waiting for transfers between devices: 72.2 us -> none  [shards(): gram = lax.psum(partial_block, 'domain')]
    all_gather x0 -> x1, waiting for transfers between devices: none -> 49.2 us  [shards(): gram = jnp.sum(lax.all_gather(partial_block, 'domain'), axis=0)]
where the time goes in v1:
time: 373 us; the launch traced here: 370 us
  waiting for transfers between devices  233 us (62%)
  matrix products  58.6 us (16%)
  starting transfers between devices  30 us (8%)
  local copies, waits for them, and re-layouts  16.7 us (4%)
  other arithmetic  16.5 us (4%)
  between operations  15 us (4%)
    ppermute x12, waiting for transfers between devices, from_behind(): return lax.ppermute(block, axis, route)  119 us
    all_gather x1, waiting for transfers between devices, shards(): gathered = lax.all_gather(filtered, 'vec', axis=1, tiled=True)  64.1 us
    all_gather x1, waiting for transfers between devices, shards(): gram = jnp.sum(lax.all_gather(partial_block, 'domain'), axis=0)  49.2 us
    ppermute x12, starting transfers between devices, from_behind(): return lax.ppermute(block, axis, route)  29.9 us
    dot_general x9, matrix products, block_step(): jnp.einsum('tji,tjc->tic', tile, own[rloc], precision=lax.Precision.HIGHEST)  18.5 us
    dot_general x9, matrix products, block_step(): jnp.einsum('tij,tjc->tic', tile, window[cloc], precision=lax.Precision.HI...  15.2 us
    dot_general x9, matrix products, block_step(): jnp.einsum('tg,tic->gic', col_hot, back, precision=lax.Precision.HIGHEST)  13.5 us
    dot_general x9, matrix products, block_step(): jnp.einsum('tg,tic->gic', row_hot, fwd, precision=lax.Precision.HIGHEST)  8.57 us
  transfers between devices with their start and end apart: 14, of which 8 were waited for; matrix products, arithmetic and copies ran while one was open for 3% of the time, Pallas kernels for 0%

profile of v1, /device:TPU:0, one launch (start us, length us, event | category | flops | bytes accessed | tf_op | source)
XLA Modules:
  0.0 370.3 jit_solution(11295340561699356230)
XLA Ops:
  9.8 5.6 %copy.6 = f32[64,128,128]{1,2,0:T(8,128)} copy(f32[64,128,128]{2,1,0:T(8,128)} %param.11) | data formatting | bytes 8388608 | tf_op args[1]
  15.4 5.9 %fusion.61 = f32[64,128,128]{2,1,0:T(8,128)} fusion(f32[64,128,128]{2,1,0:T(8,128)} %param.11, f32[64,128,128]{1,2,0:T(8,128)} %copy.6, pred[64]{0:T(512)(128)(4,1)S(1)} %compare_bitcast_fusion), kind=kLoop, calls=%fused_computation.98 | loop fusion | flops 3145728 | bytes 12582976 | tf_op jit(solution)/shard_map/jit(_where)/select_n | solution.py:73
  22.3 24.5 %while.36 = (s32[]{:T(128)}, f32[4,128,128]{2,0,1:T(4,128)S(1)}, f32[12,128,128]{2,0,1:T(8,128)S(1)}, s32[]{:T(128)}, s32[64]{0:T(128)S(1)}, /*index=5*/s32[]{:T...) while((s32[]{:T(128)}, f32[4,128,128]{2,0,1:T(4,128)S(1)}, ...), condition=%wide.region_1.2_spmd, body=%wide.region_0.1_spmd.sunk | while | flops 428083552 | bytes 8397583 | solution.py:50
  23.6 1.7 fusion.116
  26.9 2.1 fusion.117
  29.0 1.5 convolution_add_fusion.13
  31.8 1.7 fusion.116
  35.1 2.1 fusion.117
  37.1 1.5 convolution_add_fusion.13
  40.0 1.7 fusion.116
  43.2 2.1 fusion.117
  45.3 1.5 convolution_add_fusion.13
  46.9 1.3 collective-permute-start.3
  48.2 5.6 %collective-permute-start.2 = (f32[4,128,128]{2,0,1:T(4,128)S(1)}, f32[4,128,128]{2,0,1:T(4,128)S(1)}, u32[]{:S(2)}, u32[]{:S(2)}) collective-permute-start(f32[4,128,128]{2,0,1:T(4,128)S(1)} %get-tuple-element.252), channel_id=1, source_target_pairs={{0,4},{4,8},{8,12},{12,16},{16,20},{20,24},{24,28},{1,5},{5,9},{9,... | collective-permute-start | bytes 786440 | tf_op jit(solution)/shard_map/ppermute | solution.py:15
  54.7 4.6 %collective-permute-done.2 = f32[4,128,128]{2,0,1:T(4,128)S(1)} collective-permute-done((f32[4,128,128]{2,0,1:T(4,128)S(1)}, f32[4,128,128]{2,0,1:T(4,128)S(1)}, u32[]{:S(2)}, u32[]{:S(2)}) %collective-permute-start.2) | collective-permute-done | bytes 262176 | tf_op jit(solution)/shard_map/ppermute | solution.py:15
  59.5 1.3 collective-permute-start.5
  62.1 51.8 %collective-permute-done.5 = f32[4,128,128]{2,1,0:T(8,128)S(1)} collective-permute-done((f32[4,128,128]{2,1,0:T(8,128)S(1)}, f32[4,128,128]{2,1,0:T(8,128)S(1)}, u32[]{:S(2)}, u32[]{:S(2)}) %collective-permute-start.5) | collective-permute-done | bytes 262176 | tf_op jit(solution)/shard_map/ppermute | solution.py:15
  114.1 24.5 %while.37 = (s32[]{:T(128)}, f32[4,128,128]{2,0,1:T(4,128)S(1)}, f32[12,128,128]{2,0,1:T(8,128)S(1)}, s32[]{:T(128)}, s32[64]{0:T(128)S(1)}, /*index=5*/s32[]{:T...) while((s32[]{:T(128)}, f32[4,128,128]{2,0,1:T(4,128)S(1)}, ...), condition=%wide.region_3.4_spmd, body=%wide.region_2.3_spmd.sunk | while | flops 428083552 | bytes 8397583 | solution.py:50
  115.4 1.7 fusion.126
  118.7 2.1 fusion.127
  120.8 1.5 convolution_add_fusion.15
  123.6 1.7 fusion.126
  126.9 2.1 fusion.127
  128.9 1.5 convolution_add_fusion.15
  131.8 1.7 fusion.126
  135.0 2.1 fusion.127
  137.1 1.5 convolution_add_fusion.15
  138.7 1.3 collective-permute-start.7
  140.0 6.4 %collective-permute-start.6 = (f32[4,128,128]{2,0,1:T(4,128)S(1)}, f32[4,128,128]{2,0,1:T(4,128)S(1)}, u32[]{:S(2)}, u32[]{:S(2)}) collective-permute-start(f32[4,128,128]{2,0,1:T(4,128)S(1)} %get-tuple-element.250), channel_id=1, source_target_pairs={{0,4},{4,8},{8,12},{12,16},{16,20},{20,24},{24,28},{1,5},{5,9},{9,... | collective-permute-start | bytes 786440 | tf_op jit(solution)/shard_map/ppermute | solution.py:15
  146.5 3.8 %collective-permute-done.6 = f32[4,128,128]{2,0,1:T(4,128)S(1)} collective-permute-done((f32[4,128,128]{2,0,1:T(4,128)S(1)}, f32[4,128,128]{2,0,1:T(4,128)S(1)}, u32[]{:S(2)}, u32[]{:S(2)}) %collective-permute-start.6) | collective-permute-done | bytes 262176 | tf_op jit(solution)/shard_map/ppermute | solution.py:15
  153.2 54.4 %collective-permute-done.9 = f32[4,128,128]{2,1,0:T(8,128)S(1)} collective-permute-done((f32[4,128,128]{2,1,0:T(8,128)S(1)}, f32[4,128,128]{2,1,0:T(8,128)S(1)}, u32[]{:S(2)}, u32[]{:S(2)}) %collective-permute-start.9) | collective-permute-done | bytes 262176 | tf_op jit(solution)/shard_map/ppermute | solution.py:15
  207.7 24.7 %while.38 = (s32[]{:T(128)}, f32[4,128,128]{2,0,1:T(4,128)S(1)}, f32[12,128,128]{2,0,1:T(8,128)S(1)}, s32[]{:T(128)}, s32[64]{0:T(128)S(1)}, /*index=5*/s32[]{:T...) while((s32[]{:T(128)}, f32[4,128,128]{2,0,1:T(4,128)S(1)}, ...), condition=%wide.region_5.6_spmd, body=%wide.region_4.5_spmd.sunk | while | flops 428083552 | bytes 8397583 | solution.py:50
  209.3 1.7 fusion.136
  212.5 2.1 fusion.137
  214.6 1.5 convolution_add_fusion.17
  217.4 1.7 fusion.136
  220.7 2.1 fusion.137
  222.8 1.5 convolution_add_fusion.17
  225.6 1.7 fusion.136
  228.9 2.1 fusion.137
  230.9 1.5 convolution_add_fusion.17
  232.5 1.3 collective-permute-start.11
  233.9 6.2 %collective-permute-start.10 = (f32[4,128,128]{2,0,1:T(4,128)S(1)}, f32[4,128,128]{2,0,1:T(4,128)S(1)}, u32[]{:S(2)}, u32[]{:S(2)}) collective-permute-start(f32[4,128,128]{2,0,1:T(4,128)S(1)} %get-tuple-element.248), channel_id=1, source_target_pairs={{0,4},{4,8},{8,12},{12,16},{16,20},{20,24},{24,28},{1,5},{5,9},{9,... | collective-permute-start | bytes 786440 | tf_op jit(solution)/shard_map/ppermute | solution.py:15
  240.1 3.8 %collective-permute-done.10 = f32[4,128,128]{2,0,1:T(4,128)S(1)} collective-permute-done((f32[4,128,128]{2,0,1:T(4,128)S(1)}, f32[4,128,128]{2,0,1:T(4,128)S(1)}, u32[]{:S(2)}, u32[]{:S(2)}) %collective-permute-start.10) | collective-permute-done | bytes 262176 | tf_op jit(solution)/shard_map/ppermute | solution.py:15
  244.9 64.1 %all-gather.4.cloned.1.call-done = f32[512,512]{1,0:T(8,128)} async-done(((f32[512,128]{1,0:T(8,128)}), f32[512,512]{1,0:T(8,128)}) %all-gather.4.cloned.1.call-update) | async-done | bytes 1048592 | tf_op jit(solution)/shard_map/all_gather | solution.py:92
  308.9 2.8 convolution_multiply_fusion
  311.7 49.2 %all-gather.6.cloned.1.call-done = f32[1024,512]{1,0:T(8,128)} async-done(((f32[128,512]{1,0:T(8,128)}), f32[1024,512]{1,0:T(8,128)}) %all-gather.6.cloned.1.call-update) | async-done | bytes 2097168 | tf_op jit(solution)/shard_map/all_gather | solution.py:102
  361.0 2.5 reduce_sum.9
  (106 shorter events, 35.2 us)
Async XLA Ops:
  7.2 301.8 %all-gather.4.cloned.1.call-start = ((), (), s32[]{:S(2)}) async-start(), calls=%async_computation | async-start | bytes 1310720 | tf_op jit(solution)/shard_map/all_gather | solution.py:92
  7.2 8.2 %copy-start.1 = (s32[64,2]{0,1:T(2,128)S(1)}, s32[64,2]{0,1:T(2,128)}, u32[]{:S(2)}) copy-start(s32[64,2]{0,1:T(2,128)} %param.12) | copy-start | bytes 1540
  7.2 14.9 %collective-permute-start.1 = (f32[4,128,128]{2,1,0:T(8,128)}, f32[4,128,128]{2,1,0:T(8,128)S(1)}, u32[]{:S(2)}, u32[]{:S(2)}) collective-permute-start(f32[4,128,128]{2,1,0:T(8,128)} %bitcast.90), channel_id=1, source_target_pairs={{8,0},{12,4},{16,8},{20,12},{24,16},{28,20},{9,1},{13,5},{17,9},{2... | collective-permute-start | bytes 786440 | tf_op jit(solution)/shard_map/ppermute | solution.py:15
  8.5 13.6 %collective-permute-start = (f32[4,128,128]{2,1,0:T(8,128)}, f32[4,128,128]{2,1,0:T(8,128)S(1)}, u32[]{:S(2)}, u32[]{:S(2)}) collective-permute-start(f32[4,128,128]{2,1,0:T(8,128)} %bitcast.91), channel_id=1, source_target_pairs={{4,0},{8,4},{12,8},{16,12},{20,16},{24,20},{28,24},{5,1},{9,5},{13... | collective-permute-start | bytes 786440 | tf_op jit(solution)/shard_map/ppermute | solution.py:15
  15.4 6.7 %copy-start = (f32[512,128]{1,0:T(8,128)S(1)}, f32[512,128]{1,0:T(8,128)}, u32[]{:S(2)}) copy-start(f32[512,128]{1,0:T(8,128)} %param.10) | copy-start | bytes 786436
  46.9 7.8 %collective-permute-start.3 = (f32[4,128,128]{2,0,1:T(4,128)S(1)}, f32[4,128,128]{2,0,1:T(4,128)S(1)}, u32[]{:S(2)}, u32[]{:S(2)}) collective-permute-start(f32[4,128,128]{2,0,1:T(4,128)S(1)} %get-tuple-element.253), channel_id=1, source_target_pairs={{0,8},{4,12},{8,16},{12,20},{16,24},{20,28},{1,9},{5,13},{9,17},{1... | collective-permute-start | bytes 786440 | tf_op jit(solution)/shard_map/ppermute | solution.py:15
  48.2 11.1 %collective-permute-start.2 = (f32[4,128,128]{2,0,1:T(4,128)S(1)}, f32[4,128,128]{2,0,1:T(4,128)S(1)}, u32[]{:S(2)}, u32[]{:S(2)}) collective-permute-start(f32[4,128,128]{2,0,1:T(4,128)S(1)} %get-tuple-element.252), channel_id=1, source_target_pairs={{0,4},{4,8},{8,12},{12,16},{16,20},{20,24},{24,28},{1,5},{5,9},{9,... | collective-permute-start | bytes 786440 | tf_op jit(solution)/shard_map/ppermute | solution.py:15
  59.5 54.4 %collective-permute-start.5 = (f32[4,128,128]{2,1,0:T(8,128)S(1)}, f32[4,128,128]{2,1,0:T(8,128)S(1)}, u32[]{:S(2)}, u32[]{:S(2)}) collective-permute-start(f32[4,128,128]{2,1,0:T(8,128)S(1)} %bitcast.84), channel_id=1, source_target_pairs={{8,0},{12,4},{16,8},{20,12},{24,16},{28,20},{9,1},{13,5},{17,9},{2... | collective-permute-start | bytes 786440 | tf_op jit(solution)/shard_map/ppermute | solution.py:15
  60.8 53.1 %collective-permute-start.4 = (f32[4,128,128]{2,1,0:T(8,128)S(1)}, f32[4,128,128]{2,1,0:T(8,128)S(1)}, u32[]{:S(2)}, u32[]{:S(2)}) collective-permute-start(f32[4,128,128]{2,1,0:T(8,128)S(1)} %bitcast.85), channel_id=1, source_target_pairs={{4,0},{8,4},{12,8},{16,12},{20,16},{24,20},{28,24},{5,1},{9,5},{13... | collective-permute-start | bytes 786440 | tf_op jit(solution)/shard_map/ppermute | solution.py:15
  138.7 7.8 %collective-permute-start.7 = (f32[4,128,128]{2,0,1:T(4,128)S(1)}, f32[4,128,128]{2,0,1:T(4,128)S(1)}, u32[]{:S(2)}, u32[]{:S(2)}) collective-permute-start(f32[4,128,128]{2,0,1:T(4,128)S(1)} %get-tuple-element.251), channel_id=1, source_target_pairs={{0,8},{4,12},{8,16},{12,20},{16,24},{20,28},{1,9},{5,13},{9,17},{1... | collective-permute-start | bytes 786440 | tf_op jit(solution)/shard_map/ppermute | solution.py:15
  140.0 10.3 %collective-permute-start.6 = (f32[4,128,128]{2,0,1:T(4,128)S(1)}, f32[4,128,128]{2,0,1:T(4,128)S(1)}, u32[]{:S(2)}, u32[]{:S(2)}) collective-permute-start(f32[4,128,128]{2,0,1:T(4,128)S(1)} %get-tuple-element.250), channel_id=1, source_target_pairs={{0,4},{4,8},{8,12},{12,16},{16,20},{20,24},{24,28},{1,5},{5,9},{9,... | collective-permute-start | bytes 786440 | tf_op jit(solution)/shard_map/ppermute | solution.py:15
  150.6 57.0 %collective-permute-start.9 = (f32[4,128,128]{2,1,0:T(8,128)S(1)}, f32[4,128,128]{2,1,0:T(8,128)S(1)}, u32[]{:S(2)}, u32[]{:S(2)}) collective-permute-start(f32[4,128,128]{2,1,0:T(8,128)S(1)} %bitcast.96), channel_id=1, source_target_pairs={{8,0},{12,4},{16,8},{20,12},{24,16},{28,20},{9,1},{13,5},{17,9},{2... | collective-permute-start | bytes 786440 | tf_op jit(solution)/shard_map/ppermute | solution.py:15
  151.9 55.7 %collective-permute-start.8 = (f32[4,128,128]{2,1,0:T(8,128)S(1)}, f32[4,128,128]{2,1,0:T(8,128)S(1)}, u32[]{:S(2)}, u32[]{:S(2)}) collective-permute-start(f32[4,128,128]{2,1,0:T(8,128)S(1)} %bitcast.97), channel_id=1, source_target_pairs={{4,0},{8,4},{12,8},{16,12},{20,16},{24,20},{28,24},{5,1},{9,5},{13... | collective-permute-start | bytes 786440 | tf_op jit(solution)/shard_map/ppermute | solution.py:15
  232.5 7.5 %collective-permute-start.11 = (f32[4,128,128]{2,0,1:T(4,128)S(1)}, f32[4,128,128]{2,0,1:T(4,128)S(1)}, u32[]{:S(2)}, u32[]{:S(2)}) collective-permute-start(f32[4,128,128]{2,0,1:T(4,128)S(1)} %get-tuple-element.249), channel_id=1, source_target_pairs={{0,8},{4,12},{8,16},{12,20},{16,24},{20,28},{1,9},{5,13},{9,17},{1... | collective-permute-start | bytes 786440 | tf_op jit(solution)/shard_map/ppermute | solution.py:15
  233.9 10.1 %collective-permute-start.10 = (f32[4,128,128]{2,0,1:T(4,128)S(1)}, f32[4,128,128]{2,0,1:T(4,128)S(1)}, u32[]{:S(2)}, u32[]{:S(2)}) collective-permute-start(f32[4,128,128]{2,0,1:T(4,128)S(1)} %get-tuple-element.248), channel_id=1, source_target_pairs={{0,4},{4,8},{8,12},{12,16},{16,20},{20,24},{24,28},{1,5},{5,9},{9,... | collective-permute-start | bytes 786440 | tf_op jit(solution)/shard_map/ppermute | solution.py:15
  244.8 116.2 %all-gather.6.cloned.1.call-start = ((), (), s32[]{:S(2)}) async-start(), calls=%async_computation.1 | async-start | bytes 2359296 | tf_op jit(solution)/shard_map/all_gather | solution.py:102
Sparse Core Ops, SparseCore 0:
  244.9 63.9 all-gather.3
  311.8 49.0 all-gather.5
